TPU v7x, 768 devices: a whole 4x8x12 slice. The times are simulated.
768 devices in a mesh: role: 2 (over y_hi), grp: 24 (over z, core), tp: 16 (over x, y_lo).
Axes of the slice: x: 4, y: 8 (y_hi: 2, y_lo: 4; y = y_hi * 4 + y_lo), z: 12, core: 2. Of those that a mesh axis runs over, the one named last changes fastest.
Arguments:
- learn_input: bfloat16 [98304, 8192], P(('role', 'grp', 'tp')), may hold values from -6 to 6
- grad_output: bfloat16 [98304, 8192], P(('role', 'grp', 'tp')), may hold values from -6 to 6
- factor_down: bfloat16 [64, 8192], P(None, 'tp'), may hold values from -4 to 4
- factor_up: bfloat16 [64, 8192], P(None, 'tp'), may hold values from -4 to 4
- layer_scales: float32 [80, 64], replicated, may hold values from -4 to 4
- layer_index: int32 [1], replicated, may hold values from 0 to 79
- decode_input: bfloat16 [48, 8192], P(('role', 'grp')), may hold values from -6 to 6
- base_query: bfloat16 [48, 8192], P(('role', 'grp')), may hold values from -5 to 5
- key_cache: bfloat16 [48, 1024, 1024], P(('role', 'grp'), 'tp'), may hold values from -5 to 5
- value_cache: bfloat16 [48, 1024, 1024], P(('role', 'grp'), 'tp'), may hold values from -6 to 6
- fresh_key: bfloat16 [48, 1024], P(('role', 'grp')), may hold values from -6 to 6
- fresh_value: bfloat16 [48, 1024], P(('role', 'grp')), may hold values from -6 to 6
- cache_lengths: int32 [48], P(('role', 'grp')), may hold values from 1 to 1024, 24576 in all
Outputs:
- updated_down: bfloat16 [64, 8192], P(None, 'tp')
- updated_up: bfloat16 [64, 8192], P(None, 'tp')
- updated_scales: float32 [64], replicated
- attended: bfloat16 [48, 8192], P(('role', 'grp'))
Inputs may be any that keep to these rules, and one draw needn't show every extreme that they name: `cache_lengths`: some row has exactly 1024 live positions.
All inputs are finite; a program needn't handle non-finite values. No bound on the sum of `cache_lengths` on one device may be relied on, other than what follows from the above.
Results may differ from a plain program's by a relative error of at most 0.013.
Values may be sent and summed in bfloat16 or wider, within the bound.
A program may use at most 32 MiB of HBM per device.

v0:
```python
import math

import jax
import jax.numpy as jnp
from jax import lax
from jax.sharding import PartitionSpec as P

HEADS = 64
KVH = 8
HD = 128


rate_down = 8.0
rate_up = 8.0
rate_scale = 0.1


def body(
    learn_input,
    grad_output,
    factor_down,
    factor_up,
    layer_scales,
    layer_index,
    decode_input,
    base_query,
    key_cache,
    value_cache,
    fresh_key,
    fresh_value,
    cache_lengths,
):
    token_count = learn_input.shape[0]
    model_width = learn_input.shape[1]
    rank_count = factor_down.shape[0]
    layer_scale = lax.dynamic_slice_in_dim(layer_scales, layer_index[0], 1, 0)[0]
    scale_down = 1.0 / math.sqrt(model_width)
    scale_up = 1.0 / math.sqrt(rank_count)
    contract_rank = (((1,), (1,)), ((), ()))
    contract_tokens = (((0,), (0,)), ((), ()))
    down_piece = lax.all_gather(factor_down, "tp", axis=1, tiled=True)
    up_piece = lax.all_gather(factor_up, "tp", axis=1, tiled=True)
    first = lax.dot_general(
        learn_input, down_piece, contract_rank, preferred_element_type=jnp.float32
    )
    second = lax.dot_general(
        grad_output, up_piece, contract_rank, preferred_element_type=jnp.float32
    )
    hidden = first * scale_down
    back_signal = second * scale_up
    scaled = (hidden * layer_scale).astype(jnp.bfloat16)
    back_scaled = (back_signal * layer_scale).astype(jnp.bfloat16)
    gradient_down_term = (
        lax.dot_general(
            back_scaled, learn_input, contract_tokens, preferred_element_type=jnp.float32
        )
        * scale_down
    )
    gradient_up_term = (
        lax.dot_general(scaled, grad_output, contract_tokens, preferred_element_type=jnp.float32)
        * scale_up
    )
    gradient_scale_term = jnp.sum(hidden * back_signal, axis=0)
    all_tokens = token_count * lax.axis_size("role") * lax.axis_size("grp") * lax.axis_size("tp")
    step_scale = 1.0 / math.sqrt(all_tokens)
    shard_count = lax.axis_size("tp")
    scale_tile = jnp.broadcast_to(gradient_scale_term[:, None], (rank_count, shard_count))
    down_part, up_part, scale_part = (
        lax.psum_scatter(gradient_down_term, "tp", scatter_dimension=1, tiled=True),
        lax.psum_scatter(gradient_up_term, "tp", scatter_dimension=1, tiled=True),
        lax.psum_scatter(scale_tile, "tp", scatter_dimension=1, tiled=True),
    )
    down_total, up_total, scale_total = lax.psum((down_part, up_part, scale_part), ("role", "grp"))
    new_down = (factor_down.astype(jnp.float32) - rate_down * step_scale * down_total).astype(
        jnp.bfloat16
    )
    new_up = (factor_up.astype(jnp.float32) - rate_up * step_scale * up_total).astype(jnp.bfloat16)
    new_scales = layer_scale - rate_scale * step_scale * scale_total[:, 0]
    full_down, full_up = (
        lax.all_gather(new_down, "tp", axis=1, tiled=True),
        lax.all_gather(new_up, "tp", axis=1, tiled=True),
    )
    decode_hidden = (
        lax.dot_general(decode_input, full_down, contract_rank, preferred_element_type=jnp.float32)
        * scale_down
    )
    decode_scaled = (decode_hidden * new_scales).astype(jnp.bfloat16)
    query_rows = (
        base_query.astype(jnp.float32)
        + jnp.dot(decode_scaled, full_up, preferred_element_type=jnp.float32) * scale_up
    ).astype(jnp.bfloat16)
    row_count = base_query.shape[0]
    local_positions = key_cache.shape[1]
    groups = HEADS // KVH
    key_scale = 1.0 / math.sqrt(HD)
    query_heads = query_rows.reshape(row_count, KVH, groups, HD)
    key_heads = key_cache.reshape(row_count, local_positions, KVH, HD)
    value_heads = value_cache.reshape(row_count, local_positions, KVH, HD)
    scores = (
        jnp.einsum("rkgd,rpkd->rkgp", query_heads, key_heads, preferred_element_type=jnp.float32)
        * key_scale
    )
    fresh_score = (
        jnp.einsum(
            "rkgd,rkd->rkg",
            query_heads,
            fresh_key.reshape(row_count, KVH, HD),
            preferred_element_type=jnp.float32,
        )
        * key_scale
    )
    positions = lax.axis_index("tp") * local_positions + jnp.arange(
        local_positions, dtype=jnp.int32
    )
    live_mask = (positions[None, :] < cache_lengths[:, None])[:, None, None, :]
    local_high = jnp.maximum(jnp.max(jnp.where(live_mask, scores, -1e30), axis=3), fresh_score)
    highest = lax.pmax(local_high, "tp")
    weights = jnp.where(live_mask, jnp.exp(scores - highest[..., None]), 0.0)
    denominator = jnp.sum(weights, axis=3)
    numerator = jnp.einsum(
        "rkgp,rpkd->rkgd",
        weights.astype(jnp.bfloat16),
        value_heads,
        preferred_element_type=jnp.float32,
    )
    numerator, denominator = lax.psum((numerator, denominator), "tp")
    fresh_weight = jnp.exp(fresh_score - highest)
    fresh_rounded = lax.optimization_barrier(fresh_weight.astype(jnp.bfloat16)).astype(jnp.float32)
    numerator = numerator + fresh_rounded[..., None] * fresh_value.reshape(
        row_count, KVH, 1, HD
    ).astype(jnp.float32)
    denominator = denominator + fresh_weight
    attended = (
        (numerator / denominator[..., None]).reshape(row_count, HEADS * HD).astype(jnp.bfloat16)
    )
    return (new_down, new_up, new_scales, attended)


def solution(mesh):
    in_specs = (
        P(("role", "grp", "tp"), None),
        P(("role", "grp", "tp"), None),
        P(None, "tp"),
        P(None, "tp"),
        P(),
        P(),
        P(("role", "grp"), None),
        P(("role", "grp"), None),
        P(("role", "grp"), "tp", None),
        P(("role", "grp"), "tp", None),
        P(("role", "grp"), None),
        P(("role", "grp"), None),
        P(("role", "grp")),
    )
    out_specs = (P(None, "tp"), P(None, "tp"), P(), P(("role", "grp"), None))
    return jax.shard_map(body, mesh=mesh, in_specs=in_specs, out_specs=out_specs, check_vma=False)
```

profile of v0, /device:TPU:64, one launch (start us, length us, event | category | flops | bytes accessed | tf_op | source)
XLA Modules:
  0.0 1337.5 jit_solution(1921542609622424368)
XLA Ops:
  7.2 0.7 all-gather.7.cloned.1.call-update
  8.0 0.7 all-gather.5.cloned.1.call-update
  9.4 1.3 dynamic-slice
  10.6 0.9 dynamic-slice_reduce_fusion
  11.6 92.5 %all-gather.7.cloned.1.call-done = bf16[64,8192]{1,0:T(8,128)(2,1)} async-done(((bf16[64,512]{1,0:T(8,128)(2,1)}), bf16[64,8192]{1,0:T(8,128)(2,1)}) %all-gather.7.cloned.1.call-update) | async-done | bytes 1048592 | tf_op jit(solution)/shard_map/all_gather | solution.py:41
  104.0 2.7 fusion.27
  106.7 86.3 %all-gather.5.cloned.1.call-done = bf16[64,8192]{1,0:T(8,128)(2,1)} async-done(((bf16[64,512]{1,0:T(8,128)(2,1)}), bf16[64,8192]{1,0:T(8,128)(2,1)}) %all-gather.5.cloned.1.call-update) | async-done | bytes 1048592 | tf_op jit(solution)/shard_map/all_gather | solution.py:42
  193.1 2.2 multiply_reduce_fusion
  195.3 44.2 %all-reduce = f32[64,16]{0,1:T(8,128)S(1)} all-reduce(f32[64,16]{0,1:T(8,128)S(1)} %broadcast_in_dim.31), channel_id=4, replica_groups=mesh['role'=2,'grp'=24,'tp'=16] {'tp'}, use_global_device_ids=true, to_apply=%region_5.0.clone | all-reduce | flops 1024 | bytes 8192
  239.5 0.7 constant_dynamic-slice_fusion
  240.1 117.6 %psum.37 = f32[64,1]{0,1:T(1,128)S(1)} all-reduce(f32[64,1]{0,1:T(1,128)S(1)} %constant_dynamic-slice_fusion), channel_id=1, replica_groups=mesh['role'=2,'grp'=24,'tp'=16] {'role','grp'}, use_global_device_ids=true, to_apply=%region_6.0 | all-reduce | flops 64 | bytes 512 | tf_op jit(solution)/shard_map/psum | solution.py:73
  357.7 3.4 convolution_multiply_fusion.1
  361.2 1.8 convolution_multiply_fusion
  363.2 91.4 %reduce-scatter.3.cloned.1.call-done = f32[64,512]{1,0:T(8,128)} async-done(((f32[64,8192]{1,0:T(8,128)}), f32[64,512]{1,0:T(8,128)}) %reduce-scatter.3.cloned.1.call-update) | async-done | bytes 131088 | tf_op jit(solution)/shard_map/reduce_scatter | solution.py:69
  454.6 96.7 %reduce-scatter.5.cloned.1.call-done = f32[64,512]{1,0:T(8,128)} async-done(((f32[64,8192]{1,0:T(8,128)}), f32[64,512]{1,0:T(8,128)}) %reduce-scatter.5.cloned.1.call-update) | async-done | bytes 131088 | tf_op jit(solution)/shard_map/reduce_scatter | solution.py:70
  551.3 477.2 %all-reduce.5.cloned.1.call-done = (f32[64,512]{1,0:T(8,128)}, f32[64,512]{1,0:T(8,128)}) async-done(((f32[64,512]{1,0:T(8,128)}, f32[64,512]{1,0:T(8,128)}), (f32[64,512]{1,0:T(8,128)}, f32[64,512]{1,0:T(8,128)})) %all-reduce.5.cloned.1.call-update) | async-done | bytes 262160 | tf_op jit(solution)/shard_map/psum | solution.py:73
  1028.6 1.6 subtract_convert_fusion
  1030.2 1.6 subtract_convert_fusion.1
  1032.6 86.0 %all-gather.11.cloned.1.call-done = bf16[64,8192]{1,0:T(8,128)(2,1)} async-done(((bf16[64,512]{1,0:T(8,128)(2,1)}), bf16[64,8192]{1,0:T(8,128)(2,1)}) %all-gather.11.cloned.1.call-update) | async-done | bytes 1048592 | tf_op jit(solution)/shard_map/all_gather | solution.py:81
  1118.6 89.9 %all-gather.9.cloned.1.call-done = bf16[64,8192]{1,0:T(8,128)(2,1)} async-done(((bf16[64,512]{1,0:T(8,128)(2,1)}), bf16[64,8192]{1,0:T(8,128)(2,1)}) %all-gather.9.cloned.1.call-update) | async-done | bytes 1048592 | tf_op jit(solution)/shard_map/all_gather | solution.py:80
  1208.5 2.4 fusion.4
  1211.4 43.4 %pmax.7 = f32[1,8,8]{2,1,0:T(8,128)S(1)} all-reduce(f32[1,8,8]{2,1,0:T(8,128)S(1)} %maximum_bitcast_fusion), channel_id=1, replica_groups=mesh['role'=2,'grp'=24,'tp'=16] {'tp'}, use_global_device_ids=true, to_apply=%region_8.9 | all-reduce | flops 64 | bytes 512 | tf_op jit(solution)/shard_map/pmax | solution.py:117
  1255.2 74.7 %all-reduce.2 = (f32[1,8,8]{2,1,0:T(8,128)S(1)}, f32[1,8,8,128]{3,2,1,0:T(8,128)S(1)}) all-reduce(f32[1,8,8]{2,1,0:T(8,128)S(1)} %bitcast.94, f32[1,8,8,128]{3,2,1,0:T(8,128)S(1)} %convolution_bitcast_fusion), channel_id=1, replica_groups=mesh['role'=2,'grp'=24,'tp'=16] {'tp'}, use_global_device_ids=true, to_apply=%region_11.12 | all-reduce | flops 8256 | bytes 66048 | tf_op jit(solution)/shard_map/psum | solution.py:126
  1330.0 0.6 copy.35
  (48 shorter events, 1.4 us)
Async XLA Ops:
  7.2 185.9 %copy-start = (bf16[128,8192]{1,0:T(8,128)(2,1)S(1)}, bf16[128,8192]{1,0:T(8,128)(2,1)}, u32[]{:S(2)}) copy-start(bf16[128,8192]{1,0:T(8,128)(2,1)} %param.14) | copy-start | bytes 6291460
  7.2 96.8 %all-gather.7.cloned.1.call-start = ((), (), s32[]{:S(2)}) async-start(), calls=%async_computation.4 | async-start | bytes 1114112 | tf_op jit(solution)/shard_map/all_gather | solution.py:41
  7.9 185.2 %all-gather.5.cloned.1.call-start = ((), (), s32[]{:S(2)}) async-start(), calls=%async_computation.2 | async-start | bytes 1114112 | tf_op jit(solution)/shard_map/all_gather | solution.py:42
  8.7 446.0 %reduce-scatter.3.cloned.1.call-start = ((), (), s32[]{:S(2)}) async-start(), calls=%async_computation.3 | async-start | bytes 2228224 | tf_op jit(solution)/shard_map/reduce_scatter | solution.py:69
  357.7 850.8 %copy-start.8 = (f32[64]{0:T(128)}, f32[64]{0:T(128)S(1)}, u32[]{:S(2)}) copy-start(f32[64]{0:T(128)S(1)} %get-tuple-element.10) | copy-start | bytes 772
  361.2 190.1 %reduce-scatter.5.cloned.1.call-start = ((), (), s32[]{:S(2)}) async-start(), calls=%async_computation.5 | async-start | bytes 2228224 | tf_op jit(solution)/shard_map/reduce_scatter | solution.py:70
  363.0 665.5 %copy-start.1 = (bf16[64,512]{1,0:T(8,128)(2,1)S(1)}, bf16[64,512]{1,0:T(8,128)(2,1)}, u32[]{:S(2)}) copy-start(bf16[64,512]{1,0:T(8,128)(2,1)} %param.16) | copy-start | bytes 196612
  363.0 667.2 %copy-start.2 = (bf16[64,512]{1,0:T(8,128)(2,1)S(1)}, bf16[64,512]{1,0:T(8,128)(2,1)}, u32[]{:S(2)}) copy-start(bf16[64,512]{1,0:T(8,128)(2,1)} %param.15) | copy-start | bytes 196612
  363.0 669.4 %copy-start.3 = (bf16[1,64,1024]{2,1,0:T(8,128)(2,1)S(1)}, bf16[1,64,1024]{2,1,0:T(8,128)(2,1)}, u32[]{:S(2)}) copy-start(bf16[1,64,1024]{2,1,0:T(8,128)(2,1)} %param.21) | copy-start | bytes 393220
  363.1 669.4 %copy-start.4 = (bf16[1,64,1024]{2,1,0:T(8,128)(2,1)S(1)}, bf16[1,64,1024]{2,1,0:T(8,128)(2,1)}, u32[]{:S(2)}) copy-start(bf16[1,64,1024]{2,1,0:T(8,128)(2,1)} %param.22) | copy-start | bytes 393220
  363.1 669.5 %copy-start.7 = (bf16[1,1024]{1,0:T(2,128)(2,1)S(1)}, bf16[1,1024]{1,0:T(2,128)(2,1)}, u32[]{:S(2)}) copy-start(bf16[1,1024]{1,0:T(2,128)(2,1)} %param.24) | copy-start | bytes 6148
  363.1 845.4 %copy-start.5 = (bf16[1,8192]{1,0:T(2,128)(2,1)S(1)}, bf16[1,8192]{1,0:T(2,128)(2,1)}, u32[]{:S(2)}) copy-start(bf16[1,8192]{1,0:T(2,128)(2,1)} %param.19) | copy-start | bytes 49156
  363.1 847.8 %copy-start.6 = (bf16[1,8192]{1,0:T(2,128)(2,1)S(1)}, bf16[1,8192]{1,0:T(2,128)(2,1)}, u32[]{:S(2)}) copy-start(bf16[1,8192]{1,0:T(2,128)(2,1)} %param.20) | copy-start | bytes 49156
  363.1 847.9 %copy-start.9 = (bf16[1,1024]{1,0:T(2,128)(2,1)S(1)}, bf16[1,1024]{1,0:T(2,128)(2,1)}, u32[]{:S(2)}) copy-start(bf16[1,1024]{1,0:T(2,128)(2,1)} %param.23) | copy-start | bytes 6148
  363.1 665.5 %all-reduce.5.cloned.1.call-start = ((), (), s32[]{:S(2)}) async-start(), calls=%async_computation.8 | async-start | bytes 524288 | tf_op jit(solution)/shard_map/psum | solution.py:73
  551.3 567.3 %all-gather.11.cloned.1.call-start = ((), (), s32[]{:S(2)}) async-start(), calls=%async_computation.7 | async-start | bytes 1114112 | tf_op jit(solution)/shard_map/all_gather | solution.py:81
  1030.2 178.3 %all-gather.9.cloned.1.call-start = ((), (), s32[]{:S(2)}) async-start(), calls=%async_computation.6 | async-start | bytes 1114112 | tf_op jit(solution)/shard_map/all_gather | solution.py:80
Sparse Core Ops, SparseCore 0:
  10.4 93.5 all-gather.6
  106.4 86.6 all-gather.4
  361.3 93.2 reduce-scatter.2
  457.6 93.6 reduce-scatter.4
  554.4 474.1 all-reduce.4
  1031.7 86.8 all-gather.10
  1121.8 86.6 all-gather.8
where the time goes:
time: 1340 us
  waiting for transfers between devices  1020 us (76%)
  blocking collectives  280 us (21%)
  between operations  15.6 us (1%)
    psum x1, waiting for transfers between devices, body(): lax.psum((down_part, up_part, scale_part), ('role', 'grp'))  477 us
    psum x1, blocking collectives, body(): lax.psum((down_part, up_part, scale_part), ('role', 'grp'))  118 us
    reduce_scatter x1, waiting for transfers between devices, body(): lax.psum_scatter(gradient_up_term, 'tp', scatter_dimension=1, tiled=True)  96.7 us
    all_gather x1, waiting for transfers between devices, body(): down_piece = lax.all_gather(factor_down, 'tp', axis=1, tiled=True)  92.5 us
    reduce_scatter x1, waiting for transfers between devices, body(): lax.psum_scatter(gradient_down_term, 'tp', scatter_dimension=1, tiled=True)  91.4 us
    all_gather x1, waiting for transfers between devices, body(): lax.all_gather(new_down, 'tp', axis=1, tiled=True)  89.9 us
    all_gather x1, waiting for transfers between devices, body(): up_piece = lax.all_gather(factor_up, 'tp', axis=1, tiled=True)  86.3 us
    all_gather x1, waiting for transfers between devices, body(): lax.all_gather(new_up, 'tp', axis=1, tiled=True)  86 us
  transfers between devices with their start and end apart: 7, of which 7 were waited for; matrix products, arithmetic and copies ran while one was open for 1% of the time, Pallas kernels for 0%

commit v1 on v0

v1 whole, which is shorter than its diff:
```python
import math

import jax
import jax.numpy as jnp
from jax import lax
from jax.experimental import pallas as pl
from jax.experimental.pallas import tpu as pltpu
from jax.sharding import PartitionSpec as P

HEADS = 64
KVH = 8
HD = 128

rate_down = 8.0
rate_up = 8.0
rate_scale = 0.1

MESH = pl.DeviceIdType.MESH
NX = 4
NY = 4
ZL = 4
F32 = jnp.float32
BF16 = jnp.bfloat16


def kernel(
    roles, grps, tps,
    learn, grad, fdown, fup, lscales, lindex, dinput, bquery, kcache, vcache, fkey, fvalue, lengths,
    ndown, nup, nscale, att,
    xbuf, fall, sx, gbuf, rc, rs_src, rs_dst, z_src, z_dst, fown, nb, dh, kv_src, kv, atb, ls, din, bq, fk, fv,
    loc, xs, xr, fs, fr, ss, sr, gs, gr, ks, kr, r3s, r3r, r4s, r4r, n5s, n5r, dhs, dhr, ats, atr,
):
    cols = fdown.shape[1]
    rank = fdown.shape[0]
    toks = learn.shape[0]
    width = learn.shape[1]
    zh_n = grps // (2 * ZL)
    role = lax.axis_index("role")
    grp = lax.axis_index("grp")
    tp = lax.axis_index("tp")
    x, ylo = tp // NY, tp % NY
    y = role * NY + ylo
    z, core = grp // 2, grp % 2
    zh, zl = z // ZL, z % ZL
    ny = roles * NY
    other = 1 - core
    sib = (role, z * 2 + other, tp)

    def plane(dx, dy, sign):
        d = dy - NY if dy == NY - 1 else dy
        xx = (x + sign * dx + NX) % NX
        yy = (y + sign * d + ny) % ny
        return (yy // NY, grp, xx * NY + yy % NY)

    offsets = [(dx, dy) for dx in range(NX) for dy in range(NY) if dx or dy]
    n_plane = len(offsets)

    def team(d):
        b = (role * ZL + zl + d) % (roles * ZL)
        return b // ZL, zh * ZL + b % ZL

    block = role * ZL + zl
    n_team = roles * ZL

    def far(e):
        return (role, (((zh + e) % zh_n) * ZL + zl) * 2 + core, tp)

    local = []

    def fetch(src, dst):
        c = pltpu.make_async_copy(src, dst, loc.at[len(local)])
        c.start()
        local.append(c)
        return c

    sends = []

    def send(src, dst, s, r, dev):
        c = pltpu.make_async_remote_copy(
            src_ref=src, dst_ref=dst, send_sem=s, recv_sem=r, device_id=dev, device_id_type=MESH
        )
        c.start()
        sends.append(c)
        return c

    @pl.when(core == 0)
    def _():
        pltpu.make_async_copy(fdown, fall.at[tp], loc.at[0]).start()
        pltpu.make_async_copy(learn, xbuf.at[core], loc.at[1]).start()

    @pl.when(core == 1)
    def _():
        pltpu.make_async_copy(fup, fall.at[tp], loc.at[0]).start()
        pltpu.make_async_copy(grad, xbuf.at[core], loc.at[1]).start()

    c_f = pltpu.make_async_copy(fdown, fall.at[tp], loc.at[0])
    c_x = pltpu.make_async_copy(learn, xbuf.at[core], loc.at[1])
    local.extend([c_f, c_x])
    c_ls = fetch(lscales, ls)
    c_din = fetch(dinput, din)
    c_bq = fetch(bquery, bq)
    c_fk = fetch(fkey, fk)
    c_fv = fetch(fvalue, fv)
    c_k = fetch(kcache.at[0], kv_src.at[0])
    c_v = fetch(vcache.at[0], kv_src.at[1])

    with jax.named_scope("greet"):
        barrier = pltpu.get_barrier_semaphore()

        def greet(dev):
            pl.semaphore_signal(barrier, inc=1, device_id=dev, device_id_type=MESH)

        for dx, dy in offsets:
            greet(plane(dx, dy, -1))
        for d in range(1, tps):
            greet((role, grp, (tp + d) % tps))
        greet(sib)
        for d in range(1, n_team):
            rr, zz = team(d)
            greet((rr, zz * 2 + core, tp))
            greet((rr, zz * 2 + other, tp))
        for e in range(1, zh_n):
            greet(far(e))
        pl.semaphore_wait(barrier, n_plane + tps - 1 + 1 + 2 * (n_team - 1) + zh_n - 1)

    with jax.named_scope("send_own"):
        @pl.when(core == 0)
        def _():
            pltpu.make_async_remote_copy(
                src_ref=grad, dst_ref=xbuf.at[core], send_sem=xs.at[0], recv_sem=xr.at[0],
                device_id=sib, device_id_type=MESH,
            ).start()

        @pl.when(core == 1)
        def _():
            pltpu.make_async_remote_copy(
                src_ref=learn, dst_ref=xbuf.at[core], send_sem=xs.at[0], recv_sem=xr.at[0],
                device_id=sib, device_id_type=MESH,
            ).start()

        c_xs = pltpu.make_async_remote_copy(
            src_ref=learn, dst_ref=xbuf.at[core], send_sem=xs.at[0], recv_sem=xr.at[0],
            device_id=sib, device_id_type=MESH,
        )
        c_f.wait()
        gathers = []
        for i, (dx, dy) in enumerate(offsets):
            gathers.append(send(fall.at[tp], fall.at[tp], fs.at[i], fr.at[i], plane(dx, dy, 1)))

    sc = jnp.where(core == 0, 1.0 / math.sqrt(width), 1.0 / math.sqrt(rank)).astype(F32)
    rate = jnp.where(core == 0, rate_down, rate_up).astype(F32)
    step_scale = 1.0 / math.sqrt(toks * roles * grps * tps)
    fown[...] = fall[tp].astype(F32).reshape(fown.shape)

    c_ls.wait()
    row_i = lax.broadcasted_iota(jnp.int32, ls.shape, 0)
    ls_row = jnp.sum(jnp.where(row_i == lindex[0], ls[...], 0.0), axis=0, keepdims=True)
    eye = lax.broadcasted_iota(jnp.int32, (rank, rank), 0) == lax.broadcasted_iota(jnp.int32, (rank, rank), 1)

    def to_col(row):
        return jnp.sum(jnp.where(eye, jnp.broadcast_to(row, (rank, rank)), 0.0), axis=1, keepdims=True)

    def to_row(col):
        return jnp.sum(jnp.where(eye, jnp.broadcast_to(col, (rank, rank)), 0.0), axis=0, keepdims=True)

    ls_col = to_col(ls_row)

    def operand(slot):
        return xbuf[:, :, pl.ds(pl.multiple_of(slot * cols, cols), cols)].reshape(2 * toks, cols)

    NT = (((1,), (1,)), ((), ()))
    with jax.named_scope("project"):
        c_x.wait()
        c_xs.wait_recv()
        acc = lax.dot_general(fall[tp], operand(tp), NT, preferred_element_type=F32)
        for i, (dx, dy) in enumerate(offsets):
            gathers[i].wait_recv()
            slot = ((x - dx + NX) % NX) * NY + (ylo - dy + NY) % NY
            acc = acc + lax.dot_general(fall[slot], operand(slot), NT, preferred_element_type=F32)
        sx[core] = acc * sc

    with jax.named_scope("swap_projection"):
        c_s = send(sx.at[core], sx.at[core], ss.at[0], sr.at[0], sib)
        c_s.wait_recv()

    with jax.named_scope("gradient"):
        term = (sx[other] * ls_col).astype(BF16)
        scatters = []
        for i, (dx, dy) in enumerate(offsets):
            dev = plane(dx, dy, 1)
            slot = dev[2]
            g = jnp.dot(term, operand(slot), preferred_element_type=F32) * sc
            gbuf[slot] = g.astype(BF16)
            scatters.append(send(gbuf.at[slot], rc.at[i], gs.at[i], gr.at[i], dev))
        total = jnp.dot(term, operand(tp), preferred_element_type=F32) * sc
        scale_row = to_row(jnp.sum(sx[0] * sx[1], axis=1, keepdims=True))

    with jax.named_scope("send_cache"):
        c_k.wait()
        c_v.wait()
        caches = []
        head = tp // 2
        kv[:, tp] = kv_src[:, :, pl.ds(pl.multiple_of(head * HD, HD), HD)]
        for d in range(1, tps):
            to = (tp + d) % tps
            his = pl.ds(pl.multiple_of((to // 2) * HD, HD), HD)
            caches.append(
                send(kv_src.at[:, :, his], kv.at[:, tp], ks.at[d - 1], kr.at[d - 1], (role, grp, to))
            )

    with jax.named_scope("sum_plane"):
        for i in range(n_plane):
            scatters[i].wait_recv()
            total = total + rc[i].astype(F32)
        rs_src[:, :, :cols] = total.reshape(n_team, rank // n_team, cols)
        wide = jnp.concatenate([scale_row, jnp.zeros_like(scale_row)], axis=1)
        rs_src[:, :, cols:] = jnp.broadcast_to(wide, (n_team, rank // n_team, 2 * rank))

    with jax.named_scope("sum_team"):
        team_c = []
        for d in range(1, n_team):
            rr, zz = team(d)
            b = (block + d) % n_team
            team_c.append(
                send(rs_src.at[b], rs_dst.at[d - 1], r3s.at[d - 1], r3r.at[d - 1], (rr, zz * 2 + core, tp))
            )
        part = rs_src[block]
        for d in range(1, n_team):
            team_c[d - 1].wait_recv()
            part = part + rs_dst[d - 1]

    with jax.named_scope("sum_far"):
        z_src[...] = part
        far_c = []
        for e in range(1, zh_n):
            far_c.append(send(z_src, z_dst.at[e - 1], r4s.at[e - 1], r4r.at[e - 1], far(e)))
        for e in range(1, zh_n):
            far_c[e - 1].wait_recv()
            part = part + z_dst[e - 1]

    with jax.named_scope("spread_factors"):
        new = fown[block] - (rate * step_scale) * part[:, :cols]
        nb[core, block] = new.astype(BF16).astype(F32)
        spread = []
        mine = nb.at[core, block]
        spread.append(send(mine, mine, n5s.at[0, 0], n5r.at[0, 0], sib))
        for d in range(1, n_team):
            rr, zz = team(d)
            spread.append(send(mine, mine, n5s.at[0, d], n5r.at[0, d], (rr, zz * 2 + core, tp)))
            spread.append(send(mine, mine, n5s.at[1, d], n5r.at[1, d], (rr, zz * 2 + other, tp)))
        c_din.wait()
        drow = jnp.broadcast_to(
            din[:, pl.ds(pl.multiple_of(tp * cols, cols), cols)].astype(F32), (16, cols)
        ).astype(BF16)
        for c in spread:
            c.wait_recv()
        new_down = nb[0].reshape(rank, cols).astype(BF16)
        new_up = nb[1].reshape(rank, cols).astype(BF16)
        ndown[...] = new_down
        nup[...] = new_up

    with jax.named_scope("decode_hidden"):
        hid = lax.dot_general(drow, new_down, NT, preferred_element_type=F32)[:1]
        dh[tp] = jnp.concatenate([hid, part[:1, cols:cols + rank]], axis=1)
        hid_c = []
        for d in range(1, tps):
            hid_c.append(send(dh.at[tp], dh.at[tp], dhs.at[d - 1], dhr.at[d - 1], (role, grp, (tp + d) % tps)))
        for c in hid_c:
            c.wait_recv()
        both = jnp.sum(dh[...], axis=0)
        scale_total = pltpu.roll(both, rank, 1)[:, :rank]
        new_scales = ls_row - (rate_scale * step_scale) * scale_total
        nscale[...] = new_scales
        dscaled = (both[:, :rank] * (1.0 / math.sqrt(width)) * new_scales)
        dscaled = jnp.broadcast_to(dscaled, (16, rank)).astype(BF16)
        c_bq.wait()
        q = jnp.dot(dscaled, new_up, preferred_element_type=F32)[:1] * (1.0 / math.sqrt(rank))
        q = bq[:, pl.ds(pl.multiple_of(tp * cols, cols), cols)].astype(F32) + q
        mine_n = cols // HD
        q = jnp.concatenate([q[:, h * HD:(h + 1) * HD] for h in range(mine_n)] + [jnp.zeros((16 - mine_n, HD), F32)], axis=0).astype(BF16)

    with jax.named_scope("attend"):
        c_fk.wait()
        c_fv.wait()
        for c in caches:
            c.wait_recv()
        hs = pl.ds(pl.multiple_of(head * HD, HD), HD)
        n_pos = tps * kv.shape[2]
        keys = kv[0].reshape(n_pos, HD)
        values = kv[1].reshape(n_pos, HD)
        key_scale = 1.0 / math.sqrt(HD)
        s = lax.dot_general(q, keys, NT, preferred_element_type=F32) * key_scale
        fresh = jnp.sum(q.astype(F32) * fk[:, hs].astype(F32), axis=1, keepdims=True) * key_scale
        live = lax.broadcasted_iota(jnp.int32, s.shape, 1) < lengths[0]
        high = jnp.maximum(jnp.max(jnp.where(live, s, -1e30), axis=1, keepdims=True), fresh)
        w = jnp.where(live, jnp.exp(s - high), 0.0)
        fw = jnp.exp(fresh - high)
        den = jnp.sum(w, axis=1, keepdims=True) + fw
        num = jnp.dot(w.astype(BF16), values, preferred_element_type=F32)
        num = num + fw.astype(BF16).astype(F32) * fv[:, hs].astype(F32)
        res = num / den
        atb[tp] = res[:mine_n]

    with jax.named_scope("spread_attended"):
        at_c = []
        for d in range(1, tps):
            at_c.append(send(atb.at[tp], atb.at[tp], ats.at[d - 1], atr.at[d - 1], (role, grp, (tp + d) % tps)))
        for c in at_c:
            c.wait_recv()
        for s_ in range(tps):
            att[s_ * mine_n:(s_ + 1) * mine_n, :] = atb[s_]

    with jax.named_scope("drain"):
        c_xs.wait_send()
        for c in sends:
            c.wait_send()


def body(*args):
    learn, grad, fdown = args[0], args[1], args[2]
    roles, grps, tps = (lax.axis_size(a) for a in ("role", "grp", "tp"))
    rank, cols = fdown.shape
    toks, width = learn.shape
    local_pos = args[8].shape[1]
    n_plane = NX * NY - 1
    n_team = roles * ZL
    zh_n = grps // (2 * ZL)
    mine_n = cols // HD
    kvw = args[10].shape[1]
    any_spec = pl.BlockSpec(memory_space=pl.ANY)
    smem = pl.BlockSpec(memory_space=pltpu.SMEM)
    vmem = pl.BlockSpec(memory_space=pltpu.VMEM)
    in_specs = [any_spec] * 5 + [smem] + [any_spec] * 6 + [smem]
    rb = rank // n_team
    dma = pltpu.SemaphoreType.DMA
    outs = pl.pallas_call(
        lambda *refs: kernel(roles, grps, tps, *refs),
        out_shape=(
            jax.ShapeDtypeStruct((rank, cols), BF16),
            jax.ShapeDtypeStruct((rank, cols), BF16),
            jax.ShapeDtypeStruct((1, rank), F32),
            jax.ShapeDtypeStruct((HEADS, HD), F32),
        ),
        in_specs=in_specs,
        out_specs=(vmem, vmem, vmem, vmem),
        scratch_shapes=[
            pltpu.VMEM((2, toks, width), BF16),
            pltpu.VMEM((tps, rank, cols), BF16),
            pltpu.VMEM((2, rank, 2 * toks), F32),
            pltpu.VMEM((tps, rank, cols), BF16),
            pltpu.VMEM((n_plane, rank, cols), BF16),
            pltpu.VMEM((n_team, rb, cols + 2 * rank), F32),
            pltpu.VMEM((n_team - 1, rb, cols + 2 * rank), F32),
            pltpu.VMEM((rb, cols + 2 * rank), F32),
            pltpu.VMEM((zh_n - 1, rb, cols + 2 * rank), F32),
            pltpu.VMEM((n_team, rb, cols), F32),
            pltpu.VMEM((2, n_team, rb, cols), F32),
            pltpu.VMEM((tps, 1, 2 * rank), F32),
            pltpu.VMEM((2, local_pos, kvw), BF16),
            pltpu.VMEM((2, tps, local_pos, HD), BF16),
            pltpu.VMEM((tps, mine_n, HD), F32),
            pltpu.VMEM(args[4].shape, F32),
            pltpu.VMEM((1, width), BF16),
            pltpu.VMEM((1, width), BF16),
            pltpu.VMEM((1, kvw), BF16),
            pltpu.VMEM((1, kvw), BF16),
            dma((9,)),
            dma((1,)), dma((1,)),
            dma((n_plane,)), dma((n_plane,)),
            dma((1,)), dma((1,)),
            dma((n_plane,)), dma((n_plane,)),
            dma((tps - 1,)), dma((tps - 1,)),
            dma((n_team - 1,)), dma((n_team - 1,)),
            dma((zh_n - 1,)), dma((zh_n - 1,)),
            dma((2, n_team)), dma((2, n_team)),
            dma((tps - 1,)), dma((tps - 1,)),
            dma((tps - 1,)), dma((tps - 1,)),
        ],
        compiler_params=pltpu.CompilerParams(
            collective_id=0, has_side_effects=True, vmem_limit_bytes=48 * 1024 * 1024
        ),
    )(*args)
    return (
        outs[0],
        outs[1],
        outs[2].reshape(rank),
        outs[3].astype(BF16).reshape(1, HEADS * HD),
    )


def solution(mesh):
    in_specs = (
        P(("role", "grp", "tp"), None),
        P(("role", "grp", "tp"), None),
        P(None, "tp"),
        P(None, "tp"),
        P(),
        P(),
        P(("role", "grp"), None),
        P(("role", "grp"), None),
        P(("role", "grp"), "tp", None),
        P(("role", "grp"), "tp", None),
        P(("role", "grp"), None),
        P(("role", "grp"), None),
        P(("role", "grp")),
    )
    out_specs = (P(None, "tp"), P(None, "tp"), P(), P(("role", "grp"), None))
    return jax.shard_map(body, mesh=mesh, in_specs=in_specs, out_specs=out_specs, check_vma=False)
```

time: 1340 us -> 115 us (0.09)
  the two profiles are of different devices: /device:TPU:64 before, /device:TPU:1 now
where the time goes in v1:
time: 115 us; the launch traced here: 112 us
  Pallas kernels  97.7 us (85%)
  local copies, waits for them, and re-layouts  12.8 us (11%)
  between operations  1.96 us (2%)
    pallas_call x1, Pallas kernels, body(): pl.pallas_call(lambda *refs: kernel(roles, grps, tps, *refs), out_shape=(...  97.7 us
    unnamed x25, local copies, waits for them, and re-layouts  12.8 us

profile of v1, /device:TPU:1, one launch (start us, length us, event | category | flops | bytes accessed | tf_op | source)
XLA Modules:
  0.0 112.4 jit_solution(2088636104898032808)
XLA Ops:
  1.9 0.8 copy.17.refs_4_
  2.8 0.0 copy-start
  2.8 1.6 %copy-done = bf16[128,8192]{1,0:T(8,128)(2,1)S(1)} copy-done((bf16[128,8192]{1,0:T(8,128)(2,1)S(1)}, bf16[128,8192]{1,0:T(8,128)(2,1)}, u32[]{:S(2)}) %copy-start) | copy-done | bytes 2097176
  4.4 0.0 copy-start.1
  4.4 1.6 %copy-done.1 = bf16[128,8192]{1,0:T(8,128)(2,1)S(1)} copy-done((bf16[128,8192]{1,0:T(8,128)(2,1)S(1)}, bf16[128,8192]{1,0:T(8,128)(2,1)}, u32[]{:S(2)}) %copy-start.1) | copy-done | bytes 2097176
  6.0 0.0 copy-start.2
  6.0 0.9 copy-done.2
  6.9 0.0 copy-start.3
  6.9 0.9 copy-done.3
  7.8 0.0 copy-start.4
  7.8 0.8 copy-done.4
  8.6 0.0 copy-start.5
  8.6 0.8 copy-done.5
  9.4 0.0 copy-start.6
  9.4 0.8 copy-done.6
  10.2 0.0 copy-start.7
  10.2 0.8 copy-done.7
  11.0 0.7 copy-done.8
  11.6 0.7 copy-done.9
  12.3 97.7 %shard_map.156 = (bf16[64,512]{1,0:T(8,128)(2,1)S(1)}, bf16[64,512]{1,0:T(8,128)(2,1)S(1)}, f32[1,64]{1,0:T(1,128)S(1)}, f32[64,128]{1,0:T(8,128)S(1)}) custom-call(bf16[128,8192]{1,0:T(8,128)(2,1)S(1)} %copy-done, bf16[128,8192]{1,0:T(8,128)(2,1)S(1)} %copy-done.1, bf16[64,512]{1,0:T(8,128)(2,1)S(1)} %copy-done.4, bf16[64,512]{1,0:T(8,128)(2,1)S(1)} %copy-done.5, ...), custom_call_target="tpu_custom_call" | custom-call | tf_op jit(solution)/shard_map/pallas_call | solution.py:336
  110.0 0.6 copy.20
  110.7 0.6 copy.26
  111.3 0.6 copy.27
  111.9 0.5 copy.28
  (3 shorter events, 0.0 us)
Async XLA Ops:
  2.8 1.6 %copy-start = (bf16[128,8192]{1,0:T(8,128)(2,1)S(1)}, bf16[128,8192]{1,0:T(8,128)(2,1)}, u32[]{:S(2)}) copy-start(bf16[128,8192]{1,0:T(8,128)(2,1)} %refs_0_.1) | copy-start | bytes 6291460
  4.4 1.6 %copy-start.1 = (bf16[128,8192]{1,0:T(8,128)(2,1)S(1)}, bf16[128,8192]{1,0:T(8,128)(2,1)}, u32[]{:S(2)}) copy-start(bf16[128,8192]{1,0:T(8,128)(2,1)} %refs_1_.1) | copy-start | bytes 6291460
  6.0 0.9 copy-start.2
  6.9 0.9 copy-start.3
  7.8 0.8 copy-start.4
  8.6 0.8 copy-start.5
  9.4 0.8 copy-start.6
  10.2 0.8 copy-start.7
  11.0 0.7 copy-start.8
  11.6 0.7 copy-start.9

commit v2 on v1

v2 whole, which is shorter than its diff:
```python
import math

import jax
import jax.numpy as jnp
from jax import lax
from jax.experimental import pallas as pl
from jax.experimental.pallas import tpu as pltpu
from jax.sharding import PartitionSpec as P

HEADS = 64
KVH = 8
HD = 128

rate_down = 8.0
rate_up = 8.0
rate_scale = 0.1

MESH = pl.DeviceIdType.MESH
NX = 4
NY = 4
ZL = 4
F32 = jnp.float32
BF16 = jnp.bfloat16


def kernel(
    roles, grps, tps,
    learn, grad, fdown, fup, lscales, lindex, dinput, bquery, kcache, vcache, fkey, fvalue, lengths,
    ndown, nup, nscale, att,
    xbuf, fall, sx, gbuf, rx, ry, p_src, ry2, rx2, rs_src, rs_dst, z_src, z_dst, nb, dh, kv_src, kv, atb, ls, din, bq, fk, fv,
    loc, xs, xr, a1s, a1r, a2s, a2r, ss, sr, c1s, c1r, c2s, c2r, ks, kr, r3s, r3r, r4s, r4r, n5s, n5r, dhs, dhr, ats, atr, oc,
):
    rank, cols = fdown.shape
    toks, width = learn.shape
    zn = grps // 2
    half = rank // 2
    quart = rank // 4
    role = lax.axis_index("role")
    grp = lax.axis_index("grp")
    tp = lax.axis_index("tp")
    x, ylo = tp // NY, tp % NY
    y = role * NY + ylo
    z, core = grp // 2, grp % 2
    ny = roles * NY
    other = 1 - core
    sib = (role, z * 2 + other, tp)

    XS = tuple(range(1, NX))

    def at_x(dx):
        return (role, grp, (x + dx + NX) % NX * NY + ylo)

    def at_y(dy):
        yy = (y + dy + ny) % ny
        return (yy // NY, grp, x * NY + yy % NY)

    def xi(dx):
        return (x + dx + NX) % NX

    def yi(dy):
        return (ylo + dy + NY) % NY

    def at_z(dz, c, dr=0):
        return ((role + dr) % roles, (z + dz + zn) % zn * 2 + c, tp)

    local = []

    def fetch(src, dst):
        c = pltpu.make_async_copy(src, dst, loc.at[len(local)])
        c.start()
        local.append(c)
        return c

    sends = []

    def copy(src, dst, s, r, dev):
        return pltpu.make_async_remote_copy(
            src_ref=src, dst_ref=dst, send_sem=s, recv_sem=r, device_id=dev, device_id_type=MESH
        )

    def send(src, dst, s, r, dev):
        c = copy(src, dst, s, r, dev)
        c.start()
        sends.append(c)
        return c

    @pl.when(core == 0)
    def _():
        pltpu.make_async_copy(fdown, fall.at[x, ylo], loc.at[0]).start()
        pltpu.make_async_copy(learn, xbuf.at[core], loc.at[1]).start()

    @pl.when(core == 1)
    def _():
        pltpu.make_async_copy(fup, fall.at[x, ylo], loc.at[0]).start()
        pltpu.make_async_copy(grad, xbuf.at[core], loc.at[1]).start()

    c_f = pltpu.make_async_copy(fdown, fall.at[x, ylo], loc.at[0])
    c_x = pltpu.make_async_copy(learn, xbuf.at[core], loc.at[1])
    local.extend([c_f, c_x])
    c_k = fetch(kcache.at[0], kv_src.at[0])
    c_v = fetch(vcache.at[0], kv_src.at[1])
    c_ls = fetch(lscales, ls)
    c_din = fetch(dinput, din)
    c_bq = fetch(bquery, bq)
    c_fk = fetch(fkey, fk)
    c_fv = fetch(fvalue, fv)

    FAR = tuple(range(ZL, zn, ZL))
    NEAR = (1, -1, 2)
    TEAM = [(dz, dr) for dr in range(roles) for dz in (0,) + NEAR if dz or dr]

    with jax.named_scope("greet"):
        barrier = pltpu.get_barrier_semaphore()

        def greet(dev):
            pl.semaphore_signal(barrier, inc=1, device_id=dev, device_id_type=MESH)

        greet(sib)
        for dy in (1, -1, 2, -2):
            greet(at_y(dy))
        for d in range(1, tps):
            greet((role, grp, (tp + d) % tps))
        for dz, dr in TEAM:
            greet(at_z(-dz, core, dr))
        for dz in NEAR:
            greet(at_z(-dz, other))
        for dz in FAR:
            greet(at_z(-dz, core))
        pl.semaphore_wait(barrier, 1 + 4 + tps - 1 + len(TEAM) + len(NEAR) + len(FAR))

    with jax.named_scope("send_own"):
        @pl.when(core == 0)
        def _():
            copy(grad, xbuf.at[core], xs.at[0], xr.at[0], sib).start()

        @pl.when(core == 1)
        def _():
            copy(learn, xbuf.at[core], xs.at[0], xr.at[0], sib).start()

        c_xs = copy(learn, xbuf.at[core], xs.at[0], xr.at[0], sib)
        c_f.wait()
        lo, hi = pl.ds(0, half), pl.ds(half, half)
        own = fall.at[x, ylo]
        ax = {dx: send(own, own, a1s.at[dx - 1], a1r.at[dx - 1], at_x(dx)) for dx in XS}
        ay = {
            1: [send(own, own, a1s.at[3], a1r.at[3], at_y(1))],
            -1: [send(own, own, a1s.at[4], a1r.at[4], at_y(-1))],
        }
        ay[2] = [
            send(fall.at[x, ylo, lo], fall.at[x, ylo, lo], a1s.at[5], a1r.at[5], at_y(2)),
            send(fall.at[x, ylo, hi], fall.at[x, ylo, hi], a1s.at[6], a1r.at[6], at_y(-2)),
        ]
        n2 = 0
        fwd = {}
        for dx, dy in zip(XS, (1, -1, 2)):
            ax[dx].wait_recv()
            parts = []
            sx_, q0, q1 = xi(-dx), pl.ds(0, quart), pl.ds(quart, quart)
            for rows, d in ((lo, 1), (lo, -1), (q0, 2), (q1, -2)):
                r = fall.at[sx_, ylo, rows]
                parts.append(send(r, r, a2s.at[n2], a2r.at[n2], at_y(d)))
                n2 += 1
            fwd[("x", dx)] = parts
            for c in ay[dy]:
                c.wait_recv()
            parts = []
            for d in XS:
                r = fall.at[x, yi(-dy), hi]
                parts.append(send(r, r, a2s.at[n2], a2r.at[n2], at_x(d)))
                n2 += 1
            fwd[("y", dy)] = parts

    sc = jnp.where(core == 0, 1.0 / math.sqrt(width), 1.0 / math.sqrt(rank)).astype(F32)
    rate = jnp.where(core == 0, rate_down, rate_up).astype(F32)
    step_scale = 1.0 / math.sqrt(toks * roles * grps * tps)

    c_ls.wait()
    lane = lax.broadcasted_iota(jnp.int32, ls.shape, 1)
    ls_col = jnp.sum(jnp.where(lane == lindex[0], ls[...], 0.0), axis=1, keepdims=True)
    eye = lax.broadcasted_iota(jnp.int32, (rank, rank), 0) == lax.broadcasted_iota(jnp.int32, (rank, rank), 1)

    def to_row(col):
        return jnp.sum(jnp.where(eye, jnp.broadcast_to(col, (rank, rank)), 0.0), axis=0, keepdims=True)

    ls_row = to_row(ls_col)

    def operand(ix, iy):
        slot = ix * NY + iy
        return xbuf[:, :, pl.ds(pl.multiple_of(slot * cols, cols), cols)].reshape(2 * toks, cols)

    NT = (((1,), (1,)), ((), ()))

    with jax.named_scope("project"):
        c_x.wait()
        c_xs.wait_recv()

        def project(ix, iy):
            return lax.dot_general(fall[ix, iy], operand(ix, iy), NT, preferred_element_type=F32)

        acc = project(x, ylo)
        for dx in XS:
            acc = acc + project(xi(-dx), ylo)
        for dy in (1, -1, 2):
            acc = acc + project(x, yi(-dy))
        for dx, dy in [(dx, dy) for dx in XS for dy in (1, -1, 2)]:
            pieces = fwd[("x", dx)]
            for c in ([pieces[0]] if dy == 1 else [pieces[1]] if dy == -1 else pieces[2:]):
                c.wait_recv()
            fwd[("y", dy)][dx - 1].wait_recv()
            acc = acc + project(xi(-dx), yi(-dy))
        sx[core] = acc * sc

    with jax.named_scope("swap_projection"):
        c_s = send(sx.at[core], sx.at[core], ss.at[0], sr.at[0], sib)
        c_s.wait_recv()

    with jax.named_scope("gradient"):
        term = (sx[other] * ls_col).astype(BF16)
        c1 = {}
        n1 = 0

        def slice_gradient(ix, iy):
            return jnp.dot(term, operand(ix, iy), preferred_element_type=F32) * sc

        def send_x(dx, dy, n):
            return [send(gbuf.at[xi(dx), yi(dy), lo], rx.at[dx - 1, yi(dy)], c1s.at[n], c1r.at[n], at_x(dx))]

        def send_y(dx, dy, n):
            if dy != 2:
                i = 0 if dy == 1 else 1
                return [send(gbuf.at[xi(dx), yi(dy), hi], ry.at[i, xi(dx)], c1s.at[n], c1r.at[n], at_y(dy))]
            r0, r1 = pl.ds(half, quart), pl.ds(half + quart, quart)
            return [
                send(gbuf.at[xi(dx), yi(2), r0], ry.at[2, xi(dx), pl.ds(0, quart)], c1s.at[n], c1r.at[n], at_y(2)),
                send(gbuf.at[xi(dx), yi(2), r1], ry.at[2, xi(dx), pl.ds(quart, quart)], c1s.at[n + 1], c1r.at[n + 1], at_y(-2)),
            ]

        got_x, got_y = [], []
        order = [(dx, dy) for dx in (2, 1, 3) for dy in (2, 1, -1)] + [(dx, 0) for dx in (2, 1, 3)] + [(0, dy) for dy in (2, 1, -1)]
        for dx, dy in order:
            gbuf[xi(dx), yi(dy)] = slice_gradient(xi(dx), yi(dy)).astype(BF16)
            if dx:
                s_ = send_x(dx, dy, n1)
                n1 += len(s_)
                got_x += s_
            if dy:
                s_ = send_y(dx, dy, n1)
                n1 += len(s_)
                got_y += s_
        mine = slice_gradient(x, ylo)
        gbuf[x, ylo] = mine.astype(BF16)
        scale_row = to_row(jnp.sum(sx[0] * sx[1], axis=1, keepdims=True))

    with jax.named_scope("sum_plane_first"):
        for c in got_x:
            c.wait_recv()
        two = []

        def x_sum(iy):
            t = gbuf[x, iy, :half].astype(F32)
            for i in range(NX - 1):
                t = t + rx[i, iy].astype(F32)
            return t

        def y_sum(ix):
            t = gbuf[ix, ylo, half:].astype(F32)
            for i in range(NY - 1):
                t = t + ry[i, ix].astype(F32)
            return t

        for i, dy in enumerate((2, 1, -1)):
            p_src[i] = x_sum(yi(dy)).astype(BF16)
        two.append(send(p_src.at[0, pl.ds(0, quart)], ry2.at[0, pl.ds(0, quart)], c2s.at[0], c2r.at[0], at_y(2)))
        two.append(send(p_src.at[0, pl.ds(quart, quart)], ry2.at[0, pl.ds(quart, quart)], c2s.at[1], c2r.at[1], at_y(-2)))
        two.append(send(p_src.at[1], ry2.at[1], c2s.at[2], c2r.at[2], at_y(1)))
        two.append(send(p_src.at[2], ry2.at[2], c2s.at[3], c2r.at[3], at_y(-1)))
        top = x_sum(ylo)
        for c in got_y:
            c.wait_recv()
        for i, dx in enumerate((2, 1, 3)):
            p_src[3 + i] = y_sum(xi(dx)).astype(BF16)
            two.append(send(p_src.at[3 + i], rx2.at[i], c2s.at[4 + i], c2r.at[4 + i], at_x(dx)))
        bottom = y_sum(x)

    with jax.named_scope("send_cache"):
        head = tp // 2
        c_k.wait()
        c_v.wait()
        caches = []
        kv[:, tp] = kv_src[:, :, pl.ds(pl.multiple_of(head * HD, HD), HD)]
        for d in range(1, tps):
            to = (tp + d) % tps
            his = pl.ds(pl.multiple_of((to // 2) * HD, HD), HD)
            caches.append(
                send(kv_src.at[:, :, his], kv.at[:, tp], ks.at[d - 1], kr.at[d - 1], (role, grp, to))
            )

    with jax.named_scope("sum_plane_second"):
        for c in two:
            c.wait_recv()
        for i in range(3):
            top = top + ry2[i].astype(F32)
            bottom = bottom + rx2[i].astype(F32)
        s_hi = scale_row.astype(BF16).astype(F32)
        wide = jnp.concatenate([s_hi, scale_row - s_hi], axis=1)
        rb = rank // ZL
        rs_src[0:2, :, :cols] = top.reshape(ZL // 2, rb, cols).astype(BF16)
        rs_src[2:4, :, :cols] = bottom.reshape(ZL // 2, rb, cols).astype(BF16)
        rs_src[:, :, cols:] = jnp.broadcast_to(wide, (ZL, rb, 2 * rank)).astype(BF16)

    zb = z % ZL
    with jax.named_scope("sum_team"):
        team_c = []
        for i, (dz, dr) in reversed(list(enumerate(TEAM))):
            team_c.append(
                send(rs_src.at[(zb + dz + ZL) % ZL], rs_dst.at[i], r3s.at[i], r3r.at[i], at_z(dz, core, dr))
            )
        team_c.reverse()
        part = rs_src[zb].astype(F32)
        for i, c in enumerate(team_c):
            c.wait_recv()
            part = part + rs_dst[i].astype(F32)

    with jax.named_scope("sum_far"):

        def pack(v):
            s = v[:, cols:]
            s = s + pltpu.roll(s, rank, 1)
            h = s.astype(BF16).astype(F32)
            first = lax.broadcasted_iota(jnp.int32, s.shape, 1) < rank
            return jnp.where(first, h, s - h)

        z_src[:, :cols] = part[:, :cols].astype(BF16)
        z_src[:, cols:] = pack(part).astype(BF16)
        far_c = []
        for i, dz in enumerate(FAR):
            far_c.append(send(z_src, z_dst.at[i], r4s.at[i], r4r.at[i], at_z(dz, core)))
        part = z_src[...].astype(F32)
        mine_old = fall[x, ylo, pl.ds(pl.multiple_of(zb * rb, rb), rb)].astype(F32)
        for i, c in enumerate(far_c):
            c.wait_recv()
            part = part + z_dst[i].astype(F32)

    with jax.named_scope("spread_factors"):
        new = mine_old - (rate * step_scale) * part[:, :cols]
        nb[core, zb] = new.astype(BF16)
        spread = []
        blk = nb.at[core, zb]
        spread.append(send(blk, blk, n5s.at[0], n5r.at[0], sib))
        for i, dz in enumerate(NEAR):
            spread.append(send(blk, blk, n5s.at[1 + i], n5r.at[1 + i], at_z(dz, core)))
            spread.append(send(blk, blk, n5s.at[4 + i], n5r.at[4 + i], at_z(dz, other)))
        c_din.wait()
        drow = jnp.broadcast_to(
            din[:, pl.ds(pl.multiple_of(tp * cols, cols), cols)].astype(F32), (16, cols)
        ).astype(BF16)
        for c in spread:
            c.wait_recv()
        new_down = nb[0].reshape(rank, cols)
        new_up = nb[1].reshape(rank, cols)
        outs = [
            pltpu.make_async_copy(nb.at[0], ndown, oc.at[0]),
            pltpu.make_async_copy(nb.at[1], nup, oc.at[1]),
        ]
        for c in outs:
            c.start()

    with jax.named_scope("decode_hidden"):
        hid = lax.dot_general(drow, new_down, NT, preferred_element_type=F32)[:1]
        scale_part = part[:1, cols:cols + 2 * rank]
        scale_part = scale_part + pltpu.roll(scale_part, rank, 1)
        dh[tp] = jnp.concatenate([hid, scale_part[:, :rank]], axis=1)
        hid_c = []
        for d in range(1, tps):
            hid_c.append(send(dh.at[tp], dh.at[tp], dhs.at[d - 1], dhr.at[d - 1], (role, grp, (tp + d) % tps)))
        for c in hid_c:
            c.wait_recv()
        both = jnp.sum(dh[...], axis=0)
        scale_total = pltpu.roll(both, rank, 1)[:, :rank]
        new_scales = ls_row - (rate_scale * step_scale) * scale_total
        nscale[...] = new_scales
        dscaled = (both[:, :rank] * (1.0 / math.sqrt(width)) * new_scales)
        dscaled = jnp.broadcast_to(dscaled, (16, rank)).astype(BF16)
        c_bq.wait()
        q = jnp.dot(dscaled, new_up, preferred_element_type=F32)[:1] * (1.0 / math.sqrt(rank))
        q = bq[:, pl.ds(pl.multiple_of(tp * cols, cols), cols)].astype(F32) + q
        mine_n = cols // HD
        q = jnp.concatenate([q[:, h * HD:(h + 1) * HD] for h in range(mine_n)] + [jnp.zeros((16 - mine_n, HD), F32)], axis=0).astype(BF16)

    with jax.named_scope("attend"):
        c_fk.wait()
        c_fv.wait()
        for c in caches:
            c.wait_recv()
        hs = pl.ds(pl.multiple_of(head * HD, HD), HD)
        n_pos = tps * kv.shape[2]
        keys = kv[0].reshape(n_pos, HD)
        values = kv[1].reshape(n_pos, HD)
        key_scale = 1.0 / math.sqrt(HD)
        s = lax.dot_general(q, keys, NT, preferred_element_type=F32) * key_scale
        fresh = jnp.sum(q.astype(F32) * fk[:, hs].astype(F32), axis=1, keepdims=True) * key_scale
        live = lax.broadcasted_iota(jnp.int32, s.shape, 1) < lengths[0]
        high = jnp.maximum(jnp.max(jnp.where(live, s, -1e30), axis=1, keepdims=True), fresh)
        w = jnp.where(live, jnp.exp(s - high), 0.0)
        fw = jnp.exp(fresh - high)
        den = jnp.sum(w, axis=1, keepdims=True) + fw
        num = jnp.dot(w.astype(BF16), values, preferred_element_type=F32)
        num = num + fw.astype(BF16).astype(F32) * fv[:, hs].astype(F32)
        res = num / den
        atb[tp] = res[:mine_n]

    with jax.named_scope("spread_attended"):
        at_c = []
        for d in range(1, tps):
            at_c.append(send(atb.at[tp], atb.at[tp], ats.at[d - 1], atr.at[d - 1], (role, grp, (tp + d) % tps)))
        for c in at_c:
            c.wait_recv()
        for i in range(tps):
            rows = atb[i].astype(BF16)
            for h in range(mine_n):
                at = (i * mine_n + h) * HD
                att[:, at:at + HD] = rows[h:h + 1, :]

    with jax.named_scope("drain"):
        c_xs.wait_send()
        for c in sends:
            c.wait_send()
        for c in outs:
            c.wait()


def place(*refs):
    n = len(refs) // 2
    copies = [pltpu.make_async_copy(refs[i], refs[n + i], refs[-1].at[i]) for i in range(n)]
    for c in copies:
        c.start()
    for c in copies:
        c.wait()


def body(*args):
    learn, grad, fdown = args[0], args[1], args[2]
    roles, grps, tps = (lax.axis_size(a) for a in ("role", "grp", "tp"))
    rank, cols = fdown.shape
    toks, width = learn.shape
    local_pos = args[8].shape[1]
    n_far = grps // 2 // ZL - 1
    n_team = roles * ZL - 1
    mine_n = cols // HD
    kvw = args[10].shape[1]
    half, quart, rb = rank // 2, rank // 4, rank // ZL
    args = list(args)
    args[4] = args[4].T
    hbm = pl.BlockSpec(memory_space=pltpu.HBM)
    smem = pl.BlockSpec(memory_space=pltpu.SMEM)
    vmem = pl.BlockSpec(memory_space=pltpu.VMEM)
    in_specs = [hbm] * 5 + [smem] + [hbm] * 6 + [smem]
    dma = pltpu.SemaphoreType.DMA
    outs = pl.pallas_call(
        lambda *refs: kernel(roles, grps, tps, *refs),
        out_shape=(
            jax.ShapeDtypeStruct((ZL, rb, cols), BF16),
            jax.ShapeDtypeStruct((ZL, rb, cols), BF16),
            jax.ShapeDtypeStruct((1, rank), F32),
            jax.ShapeDtypeStruct((1, HEADS * HD), BF16),
        ),
        in_specs=in_specs,
        out_specs=(hbm, hbm, vmem, vmem),
        scratch_shapes=[
            pltpu.VMEM((2, toks, width), BF16),
            pltpu.VMEM((NX, NY, rank, cols), BF16),
            pltpu.VMEM((2, rank, 2 * toks), F32),
            pltpu.VMEM((NX, NY, rank, cols), BF16),
            pltpu.VMEM((NX - 1, NY, half, cols), BF16),
            pltpu.VMEM((NY - 1, NX, half, cols), BF16),
            pltpu.VMEM((6, half, cols), BF16),
            pltpu.VMEM((3, half, cols), BF16),
            pltpu.VMEM((3, half, cols), BF16),
            pltpu.VMEM((ZL, rb, cols + 2 * rank), BF16),
            pltpu.VMEM((n_team, rb, cols + 2 * rank), BF16),
            pltpu.VMEM((rb, cols + 2 * rank), BF16),
            pltpu.VMEM((n_far, rb, cols + 2 * rank), BF16),
            pltpu.VMEM((2, ZL, rb, cols), BF16),
            pltpu.VMEM((tps, 1, 2 * rank), F32),
            pltpu.VMEM((2, local_pos, kvw), BF16),
            pltpu.VMEM((2, tps, local_pos, HD), BF16),
            pltpu.VMEM((tps, mine_n, HD), F32),
            pltpu.VMEM(args[4].shape, F32),
            pltpu.VMEM((1, width), BF16),
            pltpu.VMEM((1, width), BF16),
            pltpu.VMEM((1, kvw), BF16),
            pltpu.VMEM((1, kvw), BF16),
            dma((9,)),
            dma((1,)), dma((1,)),
            dma((7,)), dma((7,)),
            dma((21,)), dma((21,)),
            dma((1,)), dma((1,)),
            dma((28,)), dma((28,)),
            dma((7,)), dma((7,)),
            dma((tps - 1,)), dma((tps - 1,)),
            dma((n_team,)), dma((n_team,)),
            dma((n_far,)), dma((n_far,)),
            dma((7,)), dma((7,)),
            dma((tps - 1,)), dma((tps - 1,)),
            dma((tps - 1,)), dma((tps - 1,)),
            dma((2,)),
        ],
        compiler_params=pltpu.CompilerParams(
            collective_id=0, has_side_effects=True, vmem_limit_bytes=60 * 1024 * 1024
        ),
    )(*args)
    results = (outs[0].reshape(rank, cols), outs[1].reshape(rank, cols), outs[2], outs[3])
    n = len(results)
    results = pl.pallas_call(
        place,
        out_shape=tuple(jax.ShapeDtypeStruct(r.shape, r.dtype) for r in results),
        in_specs=[hbm] * n,
        out_specs=(vmem,) * n,
        scratch_shapes=[dma((n,))],
    )(*results)
    return (results[0], results[1], results[2].reshape(rank), results[3])


def solution(mesh):
    in_specs = (
        P(("role", "grp", "tp"), None),
        P(("role", "grp", "tp"), None),
        P(None, "tp"),
        P(None, "tp"),
        P(),
        P(),
        P(("role", "grp"), None),
        P(("role", "grp"), None),
        P(("role", "grp"), "tp", None),
        P(("role", "grp"), "tp", None),
        P(("role", "grp"), None),
        P(("role", "grp"), None),
        P(("role", "grp")),
    )
    out_specs = (P(None, "tp"), P(None, "tp"), P(), P(("role", "grp"), None))
    return jax.shard_map(body, mesh=mesh, in_specs=in_specs, out_specs=out_specs, check_vma=False)
```

time: 115 us -> 82.9 us (0.72); the launches traced: 112 us -> 82.7 us
  Pallas kernels: 97.7 us -> 80.8 us
  local copies, waits for them, and re-layouts: 12.8 us -> 0 us
    pallas_call x1, Pallas kernels: 97.7 us -> 79.2 us  [body(): pl.pallas_call(lambda *refs: kernel(roles, grps, tps, *refs), out_shape=(...]
    unnamed x25 -> x0, local copies, waits for them, and re-layouts: 12.8 us -> none
    pallas_call x0 -> x1, Pallas kernels: none -> 1.57 us  [body(): pl.pallas_call(place, out_shape=tuple((jax.ShapeDtypeStruct(r.shape, r.dt...]
where the time goes in v2:
time: 82.9 us; the launch traced here: 82.7 us
  Pallas kernels  80.8 us (97%)
  between operations  1.94 us (2%)
    pallas_call x1, Pallas kernels, body(): pl.pallas_call(lambda *refs: kernel(roles, grps, tps, *refs), out_shape=(...  79.2 us

profile of v2, /device:TPU:1, one launch (start us, length us, event | category | flops | bytes accessed | tf_op | source)
XLA Modules:
  0.0 82.7 jit_solution(1627144506954192004)
XLA Ops:
  1.9 79.2 %shard_map.156 = (bf16[4,16,512]{2,1,0:T(8,128)(2,1)}, bf16[4,16,512]{2,1,0:T(8,128)(2,1)}, f32[1,64]{1,0:T(1,128)}, bf16[1,8192]{1,0:T(2,128)(2,1)}) custom-call(bf16[128,8192]{1,0:T(8,128)(2,1)} %refs_0_.1, bf16[128,8192]{1,0:T(8,128)(2,1)} %refs_1_.1, bf16[64,512]{1,0:T(8,128)(2,1)} %refs_2_.1, bf16[64,512]{1,0:T(8,128)(2,1)} %refs_3_.1, ...), custom_call_target="tpu_custom_call" | custom-call | tf_op jit(solution)/shard_map/pallas_call | solution.py:459
  81.2 1.6 %shard_map.157 = (bf16[64,512]{1,0:T(8,128)(2,1)}, bf16[64,512]{1,0:T(8,128)(2,1)}, f32[1,64]{1,0:T(1,128)}, bf16[1,8192]{1,0:T(2,128)(2,1)}) custom-call(bf16[64,512]{1,0:T(8,128)(2,1)} %bitcast.4, bf16[64,512]{1,0:T(8,128)(2,1)} %bitcast.5, f32[1,64]{1,0:T(1,128)} %get-tuple-element.14.refs_2_, bf16[1,8192]{1,0:T(2,128)(2,1)} %get-tuple-element.15.refs_3_), custom_call_target="tpu_custom_call" | custom-call | tf_op jit(solution)/shard_map/pallas_call | solution.py:514

commit v3 on v2

--- a/solution.py
+++ b/solution.py
@@ -115,18 +115,28 @@
         def greet(dev):
             pl.semaphore_signal(barrier, inc=1, device_id=dev, device_id_type=MESH)
 
-        greet(sib)
+        for dz, dr in reversed(TEAM):
+            greet(at_z(-dz, core, dr))
+        for dz in FAR:
+            greet(at_z(-dz, core))
+        for d in range(1, tps):
+            greet((role, grp, (tp + d) % tps))
+        for dz in NEAR:
+            greet(at_z(-dz, other))
         for dy in (1, -1, 2, -2):
             greet(at_y(dy))
-        for d in range(1, tps):
-            greet((role, grp, (tp + d) % tps))
-        for dz, dr in TEAM:
-            greet(at_z(-dz, core, dr))
-        for dz in NEAR:
-            greet(at_z(-dz, other))
-        for dz in FAR:
-            greet(at_z(-dz, core))
+        greet(sib)
         pl.semaphore_wait(barrier, 1 + 4 + tps - 1 + len(TEAM) + len(NEAR) + len(FAR))
+
+    head = tp // 2
+    caches = []
+
+    def send_cache(i, ds=None):
+        for d in ds or range(1, tps):
+            to = (tp + d) % tps
+            his = pl.ds(pl.multiple_of((to // 2) * HD, HD), HD)
+            n = i * (tps - 1) + d - 1
+            caches.append(send(kv_src.at[i, :, his], kv.at[i, tp], ks.at[n], kr.at[n], (role, grp, to)))
 
     with jax.named_scope("send_own"):
         @pl.when(core == 0)
@@ -170,6 +180,11 @@
                 n2 += 1
             fwd[("y", dy)] = parts
 
+    with jax.named_scope("send_cache"):
+        c_k.wait()
+        c_v.wait()
+        kv[:, tp] = kv_src[:, :, pl.ds(pl.multiple_of(head * HD, HD), HD)]
+
     sc = jnp.where(core == 0, 1.0 / math.sqrt(width), 1.0 / math.sqrt(rank)).astype(F32)
     rate = jnp.where(core == 0, rate_down, rate_up).astype(F32)
     step_scale = 1.0 / math.sqrt(toks * roles * grps * tps)
@@ -282,19 +297,6 @@
             two.append(send(p_src.at[3 + i], rx2.at[i], c2s.at[4 + i], c2r.at[4 + i], at_x(dx)))
         bottom = y_sum(x)
 
-    with jax.named_scope("send_cache"):
-        head = tp // 2
-        c_k.wait()
-        c_v.wait()
-        caches = []
-        kv[:, tp] = kv_src[:, :, pl.ds(pl.multiple_of(head * HD, HD), HD)]
-        for d in range(1, tps):
-            to = (tp + d) % tps
-            his = pl.ds(pl.multiple_of((to // 2) * HD, HD), HD)
-            caches.append(
-                send(kv_src.at[:, :, his], kv.at[:, tp], ks.at[d - 1], kr.at[d - 1], (role, grp, to))
-            )
-
     with jax.named_scope("sum_plane_second"):
         for c in two:
             c.wait_recv()
@@ -335,6 +337,8 @@
         far_c = []
         for i, dz in enumerate(FAR):
             far_c.append(send(z_src, z_dst.at[i], r4s.at[i], r4r.at[i], at_z(dz, core)))
+        send_cache(0)
+        send_cache(1)
         part = z_src[...].astype(F32)
         mine_old = fall[x, ylo, pl.ds(pl.multiple_of(zb * rb, rb), rb)].astype(F32)
         for i, c in enumerate(far_c):
@@ -497,7 +501,7 @@
             dma((1,)), dma((1,)),
             dma((28,)), dma((28,)),
             dma((7,)), dma((7,)),
-            dma((tps - 1,)), dma((tps - 1,)),
+            dma((2 * tps - 2,)), dma((2 * tps - 2,)),
             dma((n_team,)), dma((n_team,)),
             dma((n_far,)), dma((n_far,)),
             dma((7,)), dma((7,)),

time: 82.9 us -> 75.6 us (0.912)
  Pallas kernels: 80.8 us -> 73.5 us
    pallas_call x1, Pallas kernels: 79.2 us -> 71.9 us  [body(): pl.pallas_call(lambda *refs: kernel(roles, grps, tps, *refs), out_shape=(...]
where the time goes in v3:
time: 75.6 us; the launch traced here: 75.4 us
  Pallas kernels  73.5 us (97%)
  between operations  1.94 us (3%)
    pallas_call x1, Pallas kernels, body(): pl.pallas_call(lambda *refs: kernel(roles, grps, tps, *refs), out_shape=(...  71.9 us
    pallas_call x1, Pallas kernels, body(): pl.pallas_call(place, out_shape=tuple((jax.ShapeDtypeStruct(r.shape, r.dt...  1.57 us

profile of v3, /device:TPU:1, one launch (start us, length us, event | category | flops | bytes accessed | tf_op | source)
XLA Modules:
  0.0 75.4 jit_solution(10859418105777739474)
XLA Ops:
  1.9 71.9 %shard_map.156 = (bf16[4,16,512]{2,1,0:T(8,128)(2,1)}, bf16[4,16,512]{2,1,0:T(8,128)(2,1)}, f32[1,64]{1,0:T(1,128)}, bf16[1,8192]{1,0:T(2,128)(2,1)}) custom-call(bf16[128,8192]{1,0:T(8,128)(2,1)} %refs_0_.1, bf16[128,8192]{1,0:T(8,128)(2,1)} %refs_1_.1, bf16[64,512]{1,0:T(8,128)(2,1)} %refs_2_.1, bf16[64,512]{1,0:T(8,128)(2,1)} %refs_3_.1, ...), custom_call_target="tpu_custom_call" | custom-call | tf_op jit(solution)/shard_map/pallas_call | solution.py:463
  73.8 1.6 %shard_map.157 = (bf16[64,512]{1,0:T(8,128)(2,1)}, bf16[64,512]{1,0:T(8,128)(2,1)}, f32[1,64]{1,0:T(1,128)}, bf16[1,8192]{1,0:T(2,128)(2,1)}) custom-call(bf16[64,512]{1,0:T(8,128)(2,1)} %bitcast.4, bf16[64,512]{1,0:T(8,128)(2,1)} %bitcast.5, f32[1,64]{1,0:T(1,128)} %get-tuple-element.14.refs_2_, bf16[1,8192]{1,0:T(2,128)(2,1)} %get-tuple-element.15.refs_3_), custom_call_target="tpu_custom_call" | custom-call | tf_op jit(solution)/shard_map/pallas_call | solution.py:518

commit v4 on v3

--- a/solution.py
+++ b/solution.py
@@ -250,52 +250,58 @@
                 send(gbuf.at[xi(dx), yi(2), r1], ry.at[2, xi(dx), pl.ds(quart, quart)], c1s.at[n + 1], c1r.at[n + 1], at_y(-2)),
             ]
 
-        got_x, got_y = [], []
-        order = [(dx, dy) for dx in (2, 1, 3) for dy in (2, 1, -1)] + [(dx, 0) for dx in (2, 1, 3)] + [(0, dy) for dy in (2, 1, -1)]
+        got_x, got_y = {}, {}
+        order = [(2, 2), (1, 2), (2, 1), (3, 2), (2, -1), (0, 2), (2, 0)]
+        order += [(1, 1), (3, 1), (1, -1), (3, -1), (0, 1), (1, 0), (0, -1), (3, 0)]
         for dx, dy in order:
             gbuf[xi(dx), yi(dy)] = slice_gradient(xi(dx), yi(dy)).astype(BF16)
             if dx:
                 s_ = send_x(dx, dy, n1)
                 n1 += len(s_)
-                got_x += s_
+                got_x[dx, dy] = s_
             if dy:
                 s_ = send_y(dx, dy, n1)
                 n1 += len(s_)
-                got_y += s_
+                got_y[dx, dy] = s_
         mine = slice_gradient(x, ylo)
         gbuf[x, ylo] = mine.astype(BF16)
         scale_row = to_row(jnp.sum(sx[0] * sx[1], axis=1, keepdims=True))
 
     with jax.named_scope("sum_plane_first"):
-        for c in got_x:
-            c.wait_recv()
         two = []
 
-        def x_sum(iy):
+        def x_sum(dy):
+            for i in XS:
+                for c in got_x[i, dy]:
+                    c.wait_recv()
+            iy = yi(dy)
             t = gbuf[x, iy, :half].astype(F32)
             for i in range(NX - 1):
                 t = t + rx[i, iy].astype(F32)
             return t
 
-        def y_sum(ix):
+        def y_sum(dx):
+            for i in (2, 1, -1):
+                for c in got_y[dx, i]:
+                    c.wait_recv()
+            ix = xi(dx)
             t = gbuf[ix, ylo, half:].astype(F32)
             for i in range(NY - 1):
                 t = t + ry[i, ix].astype(F32)
             return t
 
-        for i, dy in enumerate((2, 1, -1)):
-            p_src[i] = x_sum(yi(dy)).astype(BF16)
-        two.append(send(p_src.at[0, pl.ds(0, quart)], ry2.at[0, pl.ds(0, quart)], c2s.at[0], c2r.at[0], at_y(2)))
-        two.append(send(p_src.at[0, pl.ds(quart, quart)], ry2.at[0, pl.ds(quart, quart)], c2s.at[1], c2r.at[1], at_y(-2)))
-        two.append(send(p_src.at[1], ry2.at[1], c2s.at[2], c2r.at[2], at_y(1)))
-        two.append(send(p_src.at[2], ry2.at[2], c2s.at[3], c2r.at[3], at_y(-1)))
-        top = x_sum(ylo)
-        for c in got_y:
-            c.wait_recv()
-        for i, dx in enumerate((2, 1, 3)):
-            p_src[3 + i] = y_sum(xi(dx)).astype(BF16)
+        for i, (dx, dy) in enumerate(((2, 2), (1, 1), (3, -1))):
+            p_src[i] = x_sum(dy).astype(BF16)
+            if dy == 2:
+                for k, d in enumerate((2, -2)):
+                    r = pl.ds(k * quart, quart)
+                    two.append(send(p_src.at[0, r], ry2.at[0, r], c2s.at[k], c2r.at[k], at_y(d)))
+            else:
+                two.append(send(p_src.at[i], ry2.at[i], c2s.at[1 + i], c2r.at[1 + i], at_y(dy)))
+            p_src[3 + i] = y_sum(dx).astype(BF16)
             two.append(send(p_src.at[3 + i], rx2.at[i], c2s.at[4 + i], c2r.at[4 + i], at_x(dx)))
-        bottom = y_sum(x)
+        top = x_sum(0)
+        bottom = y_sum(0)
 
     with jax.named_scope("sum_plane_second"):
         for c in two:

time: 75.6 us -> 74.3 us (0.983)
  Pallas kernels: 73.5 us -> 72.2 us
    pallas_call x1, Pallas kernels: 71.9 us -> 70.6 us  [body(): pl.pallas_call(lambda *refs: kernel(roles, grps, tps, *refs), out_shape=(...]
where the time goes in v4:
time: 74.3 us; the launch traced here: 74.1 us
  Pallas kernels  72.2 us (97%)
  between operations  1.94 us (3%)
    pallas_call x1, Pallas kernels, body(): pl.pallas_call(lambda *refs: kernel(roles, grps, tps, *refs), out_shape=(...  70.6 us
    pallas_call x1, Pallas kernels, body(): pl.pallas_call(place, out_shape=tuple((jax.ShapeDtypeStruct(r.shape, r.dt...  1.57 us

profile of v4, /device:TPU:1, one launch (start us, length us, event | category | flops | bytes accessed | tf_op | source)
XLA Modules:
  0.0 74.1 jit_solution(3476587357734943174)
XLA Ops:
  1.9 70.6 %shard_map.156 = (bf16[4,16,512]{2,1,0:T(8,128)(2,1)}, bf16[4,16,512]{2,1,0:T(8,128)(2,1)}, f32[1,64]{1,0:T(1,128)}, bf16[1,8192]{1,0:T(2,128)(2,1)}) custom-call(bf16[128,8192]{1,0:T(8,128)(2,1)} %refs_0_.1, bf16[128,8192]{1,0:T(8,128)(2,1)} %refs_1_.1, bf16[64,512]{1,0:T(8,128)(2,1)} %refs_2_.1, bf16[64,512]{1,0:T(8,128)(2,1)} %refs_3_.1, ...), custom_call_target="tpu_custom_call" | custom-call | tf_op jit(solution)/shard_map/pallas_call | solution.py:469
  72.5 1.6 %shard_map.157 = (bf16[64,512]{1,0:T(8,128)(2,1)}, bf16[64,512]{1,0:T(8,128)(2,1)}, f32[1,64]{1,0:T(1,128)}, bf16[1,8192]{1,0:T(2,128)(2,1)}) custom-call(bf16[64,512]{1,0:T(8,128)(2,1)} %bitcast.4, bf16[64,512]{1,0:T(8,128)(2,1)} %bitcast.5, f32[1,64]{1,0:T(1,128)} %get-tuple-element.14.refs_2_, bf16[1,8192]{1,0:T(2,128)(2,1)} %get-tuple-element.15.refs_3_), custom_call_target="tpu_custom_call" | custom-call | tf_op jit(solution)/shard_map/pallas_call | solution.py:524
